TPU v7x, 32 devices: a whole 2x2x4 slice. The times are simulated.
32 devices in a mesh: seq: 4 (over z), fsdp: 8 (over y, x, core).
Axes of the slice: x: 2, y: 2, z: 4, core: 2. Of those that a mesh axis runs over, the one named last changes fastest.
Arguments:
- tokens: bfloat16 [8, 1024, 768], P('fsdp', 'seq'), may hold values from -12 to 12
- cotangent: bfloat16 [8, 1024, 768], P('fsdp', 'seq'), may hold values from -6 to 6
- lengths: int32 [8], P('fsdp'), may hold values from 128 to 1024, as said below
- w_attn: float32 [4, 768, 768], P(None, 'fsdp', 'seq'), may hold values from -0.8660254 to 0.8660254
- attn_first: float32 [4, 768, 768], P(None, 'fsdp', 'seq'), may hold values from -0.3 to 0.3
- attn_second: float32 [4, 768, 768], P(None, 'fsdp', 'seq'), may hold values from 1e-06 to 0.0001
- w_ffn: float32 [2, 768, 3072], P(None, 'fsdp', 'seq'), may hold values from -0.21650635 to 0.21650635
- ffn_first: float32 [2, 768, 3072], P(None, 'fsdp', 'seq'), may hold values from -0.3 to 0.3
- ffn_second: float32 [2, 768, 3072], P(None, 'fsdp', 'seq'), may hold values from 1e-06 to 0.0001
- vectors: float32 [12, 768], P(None, ('seq', 'fsdp')), may hold values from -1 to 1.5
- vec_first: float32 [12, 768], P(None, ('seq', 'fsdp')), may hold values from -0.3 to 0.3
- vec_second: float32 [12, 768], P(None, ('seq', 'fsdp')), may hold values from 1e-06 to 0.0001
Outputs:
- block_out: bfloat16 [8, 1024, 768], P('fsdp', 'seq')
- input_grad: float32 [8, 1024, 768], P('fsdp', 'seq')
- grad_attn: float32 [4, 768, 768], P(None, 'fsdp', 'seq')
- grad_ffn: float32 [2, 768, 3072], P(None, 'fsdp', 'seq')
- grad_vec: float32 [12, 768], P(None, ('seq', 'fsdp'))
- attn_new: float32 [4, 768, 768], P(None, 'fsdp', 'seq')
- attn_first_new: float32 [4, 768, 768], P(None, 'fsdp', 'seq')
- attn_second_new: float32 [4, 768, 768], P(None, 'fsdp', 'seq')
- ffn_new: float32 [2, 768, 3072], P(None, 'fsdp', 'seq')
- ffn_first_new: float32 [2, 768, 3072], P(None, 'fsdp', 'seq')
- ffn_second_new: float32 [2, 768, 3072], P(None, 'fsdp', 'seq')
- vec_new: float32 [12, 768], P(None, ('seq', 'fsdp'))
- vec_first_new: float32 [12, 768], P(None, ('seq', 'fsdp'))
- vec_second_new: float32 [12, 768], P(None, ('seq', 'fsdp'))
Inputs may be any that keep to these rules, and one draw needn't show every extreme that they name: `lengths`: in every draw one sequence has all 1024 tokens valid and one has 128.
All inputs are finite; a program needn't handle non-finite values.
Results may differ from a plain program's by a relative error of at most 0.011.
The roundings to bfloat16 on the way count: a program that leaves them out, or rounds other values in their place, can miss the bound.
Values may be sent and summed in bfloat16 or wider, within the bound.
No kernel may reach another device: no remote copies, remote signals or barrier semaphores. Data moves between devices by JAX's collectives and lax.ppermute only.
A program may use at most 128 MiB of HBM per device.

v0:
```python
import math
import jax
import jax.numpy as jnp
from jax import lax
from jax.sharding import PartitionSpec as P

HEAD = 64
STEP = 3
EPS_NORM = 1e-12
ADAM_RATE = 0.005
BETA_ONE = 0.9
BETA_TWO = 0.999
ADAM_EPS = 1e-08
WEIGHT_DECAY = 0.01


def layer_norm(values):
    center = values - jnp.mean(values, axis=-1, keepdims=True)
    inv_scale = lax.rsqrt(jnp.mean(center * center, axis=-1, keepdims=True) + EPS_NORM)
    return (center * inv_scale, inv_scale)


def norm_back(grad_normed, normed, inv_scale):
    return inv_scale * (
        grad_normed
        - jnp.mean(grad_normed, axis=-1, keepdims=True)
        - normed * jnp.mean(grad_normed * normed, axis=-1, keepdims=True)
    )


def gelu_pair(preact):
    normal_cdf = 0.5 * (1.0 + jax.scipy.special.erf(preact * (1.0 / math.sqrt(2.0))))
    density = jnp.exp(-0.5 * preact * preact) * (1.0 / math.sqrt(2.0 * math.pi))
    return (preact * normal_cdf, normal_cdf + preact * density)


def dot_right_t(left, right):
    return lax.dot_general(
        left, right, (((1,), (1,)), ((), ())), preferred_element_type=jnp.float32
    )


def head_scores(queries, keys_all, valid_len, head_size):
    row_count = queries.shape[0]
    query_heads = queries.reshape(row_count, -1, head_size)
    key_heads = keys_all.reshape(row_count, -1, head_size)
    scores = jnp.einsum("qhd,khd->hqk", query_heads, key_heads, preferred_element_type=jnp.float32)
    scores = scores * (1.0 / math.sqrt(head_size))
    position = jnp.arange(row_count, dtype=jnp.int32)
    return jnp.where(position[None, None, :] < valid_len, scores, -jnp.inf)


def attention_forward(queries, keys_all, values_all, valid_len, head_size):
    row_count = queries.shape[0]
    scores = head_scores(queries, keys_all, valid_len, head_size)
    log_total = jax.nn.logsumexp(scores, axis=-1)
    attn_probs = jnp.exp(scores - log_total[:, :, None]).astype(jnp.bfloat16)
    value_heads = values_all.reshape(row_count, -1, head_size)
    attn_mixed = jnp.einsum(
        "hqk,khd->qhd", attn_probs, value_heads, preferred_element_type=jnp.float32
    )
    return (attn_mixed.reshape(row_count, -1).astype(jnp.bfloat16), log_total)


def attention_backward(
    queries, keys_all, values_all, attn_mixed, grad_mixed, log_total, valid_len, head_size
):
    row_count = queries.shape[0]
    scale_attn = 1.0 / math.sqrt(head_size)
    scores = head_scores(queries, keys_all, valid_len, head_size)
    probs_full = jnp.exp(scores - log_total[:, :, None])
    attn_probs = probs_full.astype(jnp.bfloat16)
    query_heads = queries.reshape(row_count, -1, head_size)
    key_heads = keys_all.reshape(row_count, -1, head_size)
    value_heads = values_all.reshape(row_count, -1, head_size)
    grad_heads = grad_mixed.reshape(row_count, -1, head_size)
    mixed_heads = attn_mixed.reshape(row_count, -1, head_size)
    row_delta = jnp.sum(grad_heads.astype(jnp.float32) * mixed_heads.astype(jnp.float32), axis=-1).T
    grad_probs = jnp.einsum(
        "qhd,khd->hqk", grad_heads, value_heads, preferred_element_type=jnp.float32
    )
    grad_scores = (probs_full * (grad_probs - row_delta[:, :, None])).astype(jnp.bfloat16)
    grad_query = (
        jnp.einsum("hqk,khd->qhd", grad_scores, key_heads, preferred_element_type=jnp.float32)
        * scale_attn
    ).astype(jnp.bfloat16)
    grad_key = (
        jnp.einsum("hqk,qhd->khd", grad_scores, query_heads, preferred_element_type=jnp.float32)
        * scale_attn
    ).astype(jnp.bfloat16)
    grad_value = jnp.einsum(
        "hqk,qhd->khd", attn_probs, grad_heads, preferred_element_type=jnp.float32
    ).astype(jnp.bfloat16)
    return (
        grad_query.reshape(row_count, -1),
        grad_key.reshape(row_count, -1),
        grad_value.reshape(row_count, -1),
    )


def attend_all(qkv_heads, lengths):

    def forward_sequence(packed):
        return attention_forward(packed[0][:, 0], packed[0][:, 1], packed[0][:, 2], packed[1], HEAD)

    return lax.map(forward_sequence, (qkv_heads, lengths))


def attend_back(qkv_heads, mixed_heads, grad_heads, log_total, lengths):

    def backward_sequence(packed):
        grads = attention_backward(
            packed[0][:, 0],
            packed[0][:, 1],
            packed[0][:, 2],
            packed[1],
            packed[2],
            packed[3],
            packed[4],
            HEAD,
        )
        return jnp.stack(grads, axis=1)

    return lax.map(backward_sequence, (qkv_heads, mixed_heads, grad_heads, log_total, lengths))


def adam_step(parameter, gradient, moment_one, moment_two, decay_rate):
    one_new = BETA_ONE * moment_one + (1.0 - BETA_ONE) * gradient
    two_new = BETA_TWO * moment_two + (1.0 - BETA_TWO) * gradient * gradient
    one_hat = one_new / (1.0 - BETA_ONE**STEP)
    two_hat = two_new / (1.0 - BETA_TWO**STEP)
    update = one_hat / (jnp.sqrt(two_hat) + ADAM_EPS)
    return (parameter - ADAM_RATE * (update + decay_rate * parameter), one_new, two_new)


def on_device(
    tokens,
    cotangent,
    lengths,
    w_attn,
    attn_first,
    attn_second,
    w_ffn,
    ffn_first,
    ffn_second,
    vectors,
    vec_first,
    vec_second,
):
    seq_local, shard_len, model_width = tokens.shape
    row_count = seq_local * shard_len
    attn_rows, ffn_rows = (
        lax.all_gather(w_attn.astype(jnp.bfloat16), "fsdp", axis=1, tiled=True),
        lax.all_gather(w_ffn.astype(jnp.bfloat16), "fsdp", axis=1, tiled=True),
    )
    vec_half = lax.all_gather(vectors.astype(jnp.bfloat16), ("seq", "fsdp"), axis=1, tiled=True)
    vec_wide = lax.optimization_barrier(vec_half).astype(jnp.float32)
    zero_bias = jnp.zeros((model_width,), jnp.float32)
    bias_qkv = jnp.stack([vec_wide[0], zero_bias, vec_wide[1]])
    up_bias = vec_wide[8:12].reshape(-1)
    token_rows = tokens.reshape(row_count, model_width)
    cot_rows = cotangent.reshape(row_count, model_width).astype(jnp.float32)
    attn_w, ffn_w = (
        lax.all_gather(attn_rows, "seq", axis=2, tiled=True),
        lax.all_gather(ffn_rows, "seq", axis=2, tiled=True),
    )
    qkv = (
        jnp.einsum("rd,kde->rke", token_rows, attn_w[:3], preferred_element_type=jnp.float32)
        + bias_qkv
    ).astype(jnp.bfloat16)
    qkv_heads = lax.all_to_all(
        qkv.reshape(seq_local, shard_len, 3, model_width),
        "seq",
        split_axis=3,
        concat_axis=1,
        tiled=True,
    )
    mixed_heads, log_total = attend_all(qkv_heads, lengths)
    mixed_local = lax.all_to_all(mixed_heads, "seq", split_axis=1, concat_axis=2, tiled=True)
    mixed_rows = mixed_local.reshape(row_count, model_width)
    hidden_one = token_rows.astype(jnp.float32) + dot_right_t(mixed_rows, attn_w[3]) + vec_wide[2]
    normed_one, inv_one = layer_norm(hidden_one)
    resid_one = normed_one * vec_wide[4] + vec_wide[5]
    resid_half = resid_one.astype(jnp.bfloat16)
    preact = jnp.dot(resid_half, ffn_w[0], preferred_element_type=jnp.float32) + up_bias
    activation, gelu_slope = gelu_pair(preact)
    act_half = activation.astype(jnp.bfloat16)
    hidden_two = resid_one + dot_right_t(act_half, ffn_w[1]) + vec_wide[3]
    normed_two, inv_two = layer_norm(hidden_two)
    block_out = (normed_two * vec_wide[6] + vec_wide[7]).astype(jnp.bfloat16)
    grad_two = norm_back(cot_rows * vec_wide[6], normed_two, inv_two)
    grad_two_half = grad_two.astype(jnp.bfloat16)
    grad_pre = jnp.dot(grad_two_half, ffn_w[1], preferred_element_type=jnp.float32) * gelu_slope
    grad_pre_half = grad_pre.astype(jnp.bfloat16)
    grad_resid = grad_two + dot_right_t(grad_pre_half, ffn_w[0])
    grad_one = norm_back(grad_resid * vec_wide[4], normed_one, inv_one)
    grad_one_half = grad_one.astype(jnp.bfloat16)
    grad_mixed = jnp.dot(grad_one_half, attn_w[3], preferred_element_type=jnp.float32).astype(
        jnp.bfloat16
    )
    grad_heads = lax.all_to_all(
        grad_mixed.reshape(seq_local, shard_len, model_width),
        "seq",
        split_axis=2,
        concat_axis=1,
        tiled=True,
    )
    grad_stack = attend_back(qkv_heads, mixed_heads, grad_heads, log_total, lengths)
    grad_qkv = lax.all_to_all(grad_stack, "seq", split_axis=1, concat_axis=3, tiled=True).reshape(
        row_count, 3, model_width
    )
    input_grad = grad_one + jnp.einsum(
        "rke,kde->rd", grad_qkv, attn_w[:3], preferred_element_type=jnp.float32
    )
    attn_local = jnp.concatenate(
        [
            jnp.einsum("rd,rke->kde", token_rows, grad_qkv, preferred_element_type=jnp.float32),
            jnp.dot(grad_one_half.T, mixed_rows, preferred_element_type=jnp.float32)[None],
        ],
        axis=0,
    )
    ffn_local = jnp.stack(
        [
            jnp.dot(resid_half.T, grad_pre_half, preferred_element_type=jnp.float32),
            jnp.dot(grad_two_half.T, act_half, preferred_element_type=jnp.float32),
        ]
    )
    qkv_sums = jnp.sum(grad_qkv.astype(jnp.float32), axis=0)
    vec_local = jnp.concatenate(
        [
            jnp.stack(
                [
                    qkv_sums[0],
                    qkv_sums[2],
                    jnp.sum(grad_one, axis=0),
                    jnp.sum(grad_two, axis=0),
                    jnp.sum(grad_resid * normed_one, axis=0),
                    jnp.sum(grad_resid, axis=0),
                    jnp.sum(cot_rows * normed_two, axis=0),
                    jnp.sum(cot_rows, axis=0),
                ]
            ),
            jnp.sum(grad_pre, axis=0).reshape(4, model_width),
        ],
        axis=0,
    )
    attn_part, ffn_part, vec_part = (
        lax.psum_scatter(attn_local, "seq", scatter_dimension=2, tiled=True),
        lax.psum_scatter(ffn_local, "seq", scatter_dimension=2, tiled=True),
        lax.psum_scatter(vec_local, "seq", scatter_dimension=1, tiled=True),
    )
    attn_grad, ffn_grad, vec_grad = (
        lax.psum_scatter(attn_part, "fsdp", scatter_dimension=1, tiled=True),
        lax.psum_scatter(ffn_part, "fsdp", scatter_dimension=1, tiled=True),
        lax.psum_scatter(vec_part, "fsdp", scatter_dimension=1, tiled=True),
    )
    token_total = seq_local * shard_len * lax.axis_size("seq") * lax.axis_size("fsdp")
    grad_scale = float(token_total) ** (-0.5)
    attn_grad = attn_grad * grad_scale
    ffn_grad = ffn_grad * grad_scale
    vec_grad = vec_grad * grad_scale
    attn_new, attn_one, attn_two = adam_step(
        w_attn, attn_grad, attn_first, attn_second, WEIGHT_DECAY
    )
    ffn_new, ffn_one, ffn_two = adam_step(w_ffn, ffn_grad, ffn_first, ffn_second, WEIGHT_DECAY)
    vec_new, vec_one, vec_two = adam_step(vectors, vec_grad, vec_first, vec_second, 0.0)
    return (
        block_out.reshape(seq_local, shard_len, model_width),
        input_grad.reshape(seq_local, shard_len, model_width),
        attn_grad,
        ffn_grad,
        vec_grad,
        attn_new,
        attn_one,
        attn_two,
        ffn_new,
        ffn_one,
        ffn_two,
        vec_new,
        vec_one,
        vec_two,
    )


def solution(mesh):
    placed = (
        P("fsdp", "seq", None),
        P("fsdp", "seq", None),
        P("fsdp"),
        P(None, "fsdp", "seq"),
        P(None, "fsdp", "seq"),
        P(None, "fsdp", "seq"),
        P(None, "fsdp", "seq"),
        P(None, "fsdp", "seq"),
        P(None, "fsdp", "seq"),
        P(None, ("seq", "fsdp")),
        P(None, ("seq", "fsdp")),
        P(None, ("seq", "fsdp")),
    )
    return jax.shard_map(
        on_device,
        mesh=mesh,
        in_specs=placed,
        out_specs=(
            P("fsdp", "seq", None),
            P("fsdp", "seq", None),
            P(None, "fsdp", "seq"),
            P(None, "fsdp", "seq"),
            P(None, ("seq", "fsdp")),
            P(None, "fsdp", "seq"),
            P(None, "fsdp", "seq"),
            P(None, "fsdp", "seq"),
            P(None, "fsdp", "seq"),
            P(None, "fsdp", "seq"),
            P(None, "fsdp", "seq"),
            P(None, ("seq", "fsdp")),
            P(None, ("seq", "fsdp")),
            P(None, ("seq", "fsdp")),
        ),
        check_vma=False,
    )
```

profile of v0, /device:TPU:0, one launch (start us, length us, event | category | flops | bytes accessed | tf_op | source)
XLA Modules:
  0.0 1114.0 jit_solution(3864774587014703365)
XLA Ops:
  11.1 27.6 %all-gather.6.cloned.1.call-done = bf16[4,768,192]{2,0,1:T(4,128)(2,1)} async-done(((bf16[4,96,192]{2,0,1:T(4,128)(2,1)}), bf16[4,768,192]{2,0,1:T(4,128)(2,1)}) %all-gather.6.cloned.1.call-update) | async-done | bytes 1179664 | tf_op jit(solution)/shard_map/all_gather | solution.py:153
  38.8 4.2 copy.151
  43.0 27.2 %all-gather.10.cloned.1.call-done = bf16[2,768,768]{2,1,0:T(8,128)(2,1)} async-done(((bf16[2,96,768]{2,1,0:T(8,128)(2,1)}), bf16[2,768,768]{2,1,0:T(8,128)(2,1)}) %all-gather.10.cloned.1.call-update) | async-done | bytes 2359312 | tf_op jit(solution)/shard_map/all_gather | solution.py:154
  70.2 42.6 %all-gather = bf16[32,24,12]{1,2,0:T(8,128)(2,1)S(1)} all-gather(bf16[1,24,12]{1,2,0:T(8,128)(2,1)S(1)} %convert_bitcast_fusion.1), channel_id=1, replica_groups=mesh['seq'=4,'fsdp'=8] {'seq','fsdp'}, dimensions={0}, use_global_device_ids=true | all-gather | bytes 19008 | tf_op jit(solution)/shard_map/all_gather | solution.py:156
  113.8 47.7 %all-gather.8.cloned.1.call-done = bf16[4,768,768]{1,0,2:T(4,128)(2,1)} async-done(((bf16[4,768,192]{1,0,2:T(4,128)(2,1)}), bf16[4,768,768]{1,0,2:T(4,128)(2,1)}) %all-gather.8.cloned.1.call-update) | async-done | bytes 4718608 | tf_op jit(solution)/shard_map/all_gather | solution.py:164
  161.5 6.5 copy.200
  168.0 3.4 fusion.12
  171.4 3.7 copy.154
  175.1 3.7 all-to-all-start
  179.5 79.6 %all-to-all-done = bf16[1,256,3,768]{1,2,0,3:T(4,128)(2,1)S(1)} async-done(((bf16[1,256,3,768]{1,2,0,3:T(4,128)(2,1)}), bf16[1,256,3,768]{1,2,0,3:T(4,128)(2,1)S(1)}, u32[]{:S(2)}, u32[]{:S(2)}) %all-to-all-start) | async-done | bytes 1179680 | tf_op jit(solution)/shard_map/all_to_all | solution.py:171
  261.1 2.3 fusion.1
  263.5 3.2 exponential_reduce_fusion
  268.0 3.0 fusion
  275.1 4.0 reduce.14
  280.5 3.7 all-to-all-start.1
  284.3 6.2 slice.101
  290.5 5.4 copy.201
  295.9 10.5 all-to-all-done.1
  308.4 2.3 copy.159
  312.9 57.1 %all-gather.12.cloned.1.call-done = bf16[2,768,3072]{2,1,0:T(8,128)(2,1)} async-done(((bf16[2,768,768]{2,1,0:T(8,128)(2,1)}), bf16[2,768,3072]{2,1,0:T(8,128)(2,1)}) %all-gather.12.cloned.1.call-update) | async-done | bytes 9437200 | tf_op jit(solution)/shard_map/all_gather | solution.py:165
  370.0 3.7 multiply_convert_fusion.1
  379.1 2.5 fusion.53
  385.8 2.6 copy.162
  388.4 3.0 reduce.15
  391.5 14.5 %all_to_all.60 = bf16[4,2,24576]{2,1,0:T(2,128)(2,1)S(1)} all-to-all(bf16[4,2,24576]{2,1,0:T(2,128)(2,1)S(1)} %reshape.192), channel_id=1, replica_groups=mesh['seq'=4,'fsdp'=8] {'seq'}, dimensions={0} | all-to-all | bytes 786432 | tf_op jit(solution)/shard_map/all_to_all | solution.py:201
  407.1 5.6 convolution_convert_fusion
  412.9 7.1 multiply_convert_fusion
  420.0 2.8 fusion.20
  425.6 2.4 copy.169
  428.0 3.5 copy.168
  431.5 6.0 maximum_bitcast_fusion
  437.5 3.6 all-to-all-start.3
  441.3 3.0 convolution_bitcast_fusion.3
  444.4 44.5 %all-to-all-done.3 = bf16[1,1024,3,192]{3,2,0,1:T(4,128)(2,1)S(1)} async-done(((bf16[1,1024,3,192]{3,2,0,1:T(4,128)(2,1)}), bf16[1,1024,3,192]{3,2,0,1:T(4,128)(2,1)S(1)}, u32[]{:S(2)}, u32[]{:S(2)}) %all-to-all-start.3) | async-done | bytes 1179680 | tf_op jit(solution)/shard_map/all_to_all | solution.py:209
  490.2 3.9 copy.192
  496.4 4.3 pad_maximum_fusion.1
  501.9 2.9 convolution_bitcast_fusion
  506.4 7.0 pad_maximum_fusion
  516.7 144.4 %reduce-scatter.11.cloned.1.call-done = f32[4,768,192]{1,2,0:T(8,128)} async-done(((f32[4,768,768]{1,2,0:T(8,128)}), f32[4,768,192]{1,2,0:T(8,128)}) %reduce-scatter.11.cloned.1.call-update) | async-done | bytes 2359312 | tf_op jit(solution)/shard_map/reduce_scatter | solution.py:248
  661.1 3.1 copy.193
  664.2 3.1 reshape.176
  667.4 310.8 %reduce-scatter.13.cloned.1.call-done = f32[2,768,768]{2,1,0:T(8,128)} async-done(((f32[2,768,3072]{2,1,0:T(8,128)}), f32[2,768,768]{2,1,0:T(8,128)}) %reduce-scatter.13.cloned.1.call-update) | async-done | bytes 4718608 | tf_op jit(solution)/shard_map/reduce_scatter | solution.py:249
  980.2 4.0 fusion.18
  984.2 18.7 %reduce-scatter.19.cloned.1.call-done = f32[192,12]{1,0:T(8,128)} async-done(((f32[768,12]{1,0:T(8,128)}), f32[192,12]{1,0:T(8,128)}) %reduce-scatter.19.cloned.1.call-update) | async-done | bytes 9232
  1003.9 22.3 %all-reduce = f32[12,192]{1,0:T(8,128)S(1)} all-reduce(f32[12,192]{1,0:T(8,128)S(1)} %copy.196), channel_id=7, replica_groups=mesh['seq'=4,'fsdp'=8] {'fsdp'}, use_global_device_ids=true, to_apply=%region_24.25.clone | all-reduce | flops 2304 | bytes 18432
  1026.9 20.0 %reduce-scatter.17.cloned.1.call-done = f32[96,768]{1,0:T(8,128)} async-done(((f32[768,768]{1,0:T(8,128)}), f32[96,768]{1,0:T(8,128)}) %reduce-scatter.17.cloned.1.call-update) | async-done | bytes 294928
  1054.2 49.9 %reduce-scatter.15.cloned.1.call-done = f32[2,96,768]{2,1,0:T(8,128)} async-done(((f32[2,768,768]{2,1,0:T(8,128)}), f32[2,96,768]{2,1,0:T(8,128)}) %reduce-scatter.15.cloned.1.call-update) | async-done | bytes 589840 | tf_op jit(solution)/shard_map/reduce_scatter | solution.py:254
  1104.1 3.2 multiply_subtract_fusion
  (166 shorter events, 51.3 us)
Async XLA Ops:
  7.2 31.6 %all-gather.6.cloned.1.call-start = ((), (), s32[]{:S(2)}) async-start(), calls=%async_computation.9 | async-start | bytes 1769472 | tf_op jit(solution)/shard_map/all_gather | solution.py:153
  9.2 61.0 %copy-start.28 = (f32[12,24]{1,0:T(8,128)S(1)}, f32[12,24]{1,0:T(8,128)}, u32[]{:S(2)}) copy-start(f32[12,24]{1,0:T(8,128)} %param.21) | copy-start | bytes 3460
  9.2 61.0 %all-gather.10.cloned.1.call-start = ((), (), s32[]{:S(2)}) async-start(), calls=%async_computation.11 | async-start | bytes 2654208 | tf_op jit(solution)/shard_map/all_gather | solution.py:154
  11.1 150.4 %all-gather.8.cloned.1.call-start = ((), (), s32[]{:S(2)}) async-start(), calls=%async_computation.10 | async-start | bytes 5898240 | tf_op jit(solution)/shard_map/all_gather | solution.py:164
  43.0 327.1 %all-gather.12.cloned.1.call-start = ((), (), s32[]{:S(2)}) async-start(), calls=%async_computation.12 | async-start | bytes 11796480 | tf_op jit(solution)/shard_map/all_gather | solution.py:165
  113.0 48.4 %copy-start.26 = (bf16[768,12]{0,1:T(8,128)(2,1)}, bf16[768,12]{0,1:T(8,128)(2,1)S(1)}, u32[]{:S(2)}) copy-start(bf16[768,12]{0,1:T(8,128)(2,1)S(1)} %reshape.173) | copy-start | bytes 55300
  168.0 7.1 copy-start.12
  175.1 84.0 %all-to-all-start = ((bf16[1,256,3,768]{1,2,0,3:T(4,128)(2,1)}), bf16[1,256,3,768]{1,2,0,3:T(4,128)(2,1)S(1)}, u32[]{:S(2)}, u32[]{:S(2)}) async-start(bf16[1,256,3,768]{1,2,0,3:T(4,128)(2,1)} %copy.154), calls=%async_computation | async-start | bytes 3145728 | tf_op jit(solution)/shard_map/all_to_all | solution.py:171
  261.1 9.9 copy-start.17
  263.5 4.6 copy-start
  271.0 2.7 copy-start.1
  273.7 10.6 copy-start.10
  273.7 10.4 copy-start.27
  280.5 26.0 %all-to-all-start.1 = ((bf16[4,2,24576]{2,1,0:T(2,128)(2,1)}), bf16[4,2,24576]{2,1,0:T(2,128)(2,1)S(1)}, u32[]{:S(2)}, u32[]{:S(2)}) async-start(bf16[4,2,24576]{2,1,0:T(2,128)(2,1)} %reshape.190), calls=%async_computation.1 | async-start | bytes 786432 | tf_op jit(solution)/shard_map/all_to_all | solution.py:179
  370.0 5.7 copy-start.31
  373.8 3.5 copy-start.21
  375.7 1.8 copy-start.8
  379.1 2.5 copy-start.13
  381.6 1.7 copy-start.22
  383.6 0.9 copy-start.4
  407.1 5.7 copy-start.11
  407.1 5.8 copy-start.18
  422.7 2.0 copy-start.20
  437.5 51.4 %all-to-all-start.3 = ((bf16[1,1024,3,192]{3,2,0,1:T(4,128)(2,1)}), bf16[1,1024,3,192]{3,2,0,1:T(4,128)(2,1)S(1)}, u32[]{:S(2)}, u32[]{:S(2)}) async-start(bf16[1,1024,3,192]{3,2,0,1:T(4,128)(2,1)} %maximum_bitcast_fusion), calls=%async_computation.3 | async-start | bytes 4194304 | tf_op jit(solution)/shard_map/all_to_all | solution.py:209
  441.1 220.0 %reduce-scatter.11.cloned.1.call-start = ((), (), s32[]{:S(2)}) async-start(), calls=%async_computation.13 | async-start | bytes 11796480 | tf_op jit(solution)/shard_map/reduce_scatter | solution.py:248
  444.4 49.9 %copy-start.16 = (bf16[1,256,768]{2,1,0:T(8,128)(2,1)S(1)}, bf16[1,256,768]{2,1,0:T(8,128)(2,1)}, u32[]{:S(2)}) copy-start(bf16[1,256,768]{2,1,0:T(8,128)(2,1)} %param.12) | copy-start | bytes 1179652
  488.9 1.3 copy-start.3
  494.3 1.1 copy-start.6
  494.3 2.1 copy-start.2
  500.7 1.1 copy-start.14
  500.7 477.5 %reduce-scatter.13.cloned.1.call-start = ((), (), s32[]{:S(2)}) async-start(), calls=%async_computation.14 | async-start | bytes 23592960 | tf_op jit(solution)/shard_map/reduce_scatter | solution.py:249
  501.9 3.0 copy-start.23
  513.4 1.0 copy-start.9
  513.4 489.5 %reduce-scatter.19.cloned.1.call-start = ((), (), s32[]{:S(2)}) async-start(), calls=%async_computation.17 | async-start | bytes 491520
  516.6 530.3 %reduce-scatter.17.cloned.1.call-start = ((), (), s32[]{:S(2)}) async-start(), calls=%async_computation.16 | async-start | bytes 2654208
  667.4 310.9 %copy-start.19 = (f32[4,96,192]{2,1,0:T(8,128)S(1)}, f32[4,96,192]{2,1,0:T(8,128)}, u32[]{:S(2)}) copy-start(f32[4,96,192]{2,1,0:T(8,128)} %param.15) | copy-start | bytes 884740
  667.4 311.1 %copy-start.24 = (f32[4,96,192]{2,1,0:T(8,128)S(1)}, f32[4,96,192]{2,1,0:T(8,128)}, u32[]{:S(2)}) copy-start(f32[4,96,192]{2,1,0:T(8,128)} %param.16) | copy-start | bytes 884740
  667.4 311.3 %copy-start.25 = (f32[4,96,192]{2,1,0:T(8,128)S(1)}, f32[4,96,192]{2,1,0:T(8,128)}, u32[]{:S(2)}) copy-start(f32[4,96,192]{2,1,0:T(8,128)} %param.17) | copy-start | bytes 884740
  667.4 436.7 %reduce-scatter.15.cloned.1.call-start = ((), (), s32[]{:S(2)}) async-start(), calls=%async_computation.15 | async-start | bytes 5308416 | tf_op jit(solution)/shard_map/reduce_scatter | solution.py:254
  978.3 0.7 copy-start.32
  978.3 1.9 copy-start.5
  978.3 1.9 copy-start.7
  978.9 47.3 %copy-start.29 = (f32[12,24]{1,0:T(8,128)S(1)}, f32[12,24]{1,0:T(8,128)}, u32[]{:S(2)}) copy-start(f32[12,24]{1,0:T(8,128)} %param.22) | copy-start | bytes 3460
  978.9 47.3 %copy-start.30 = (f32[12,24]{1,0:T(8,128)S(1)}, f32[12,24]{1,0:T(8,128)}, u32[]{:S(2)}) copy-start(f32[12,24]{1,0:T(8,128)} %param.23) | copy-start | bytes 3460
  1048.2 55.9 %copy-start.15 = (f32[2,96,768]{2,1,0:T(8,128)S(1)}, f32[2,96,768]{2,1,0:T(8,128)}, u32[]{:S(2)}) copy-start(f32[2,96,768]{2,1,0:T(8,128)} %param.18) | copy-start | bytes 1769476
Sparse Core Ops, SparseCore 0:
  10.4 28.2 all-gather.5
  41.2 28.8 all-gather.9
  71.7 89.6 all-gather.7
  162.9 207.1 all-gather.11
  500.9 160.2 reduce-scatter.10
  663.3 314.8 reduce-scatter.12
  981.1 21.7 reduce-scatter.18
  1006.2 40.6 reduce-scatter.16
  1050.4 53.6 reduce-scatter.14
where the time goes:
time: 1120 us; the launch traced here: 1110 us
  waiting for transfers between devices  838 us (75%)
  blocking collectives  79.5 us (7%)
  local copies, waits for them, and re-layouts  78.1 us (7%)
  matrix products  49.4 us (4%)
  other arithmetic  41.2 us (4%)
  between operations  16.1 us (1%)
  starting transfers between devices  11.6 us (1%)
    reduce_scatter x1, waiting for transfers between devices, on_device(): lax.psum_scatter(ffn_local, 'seq', scatter_dimension=2, tiled=True)  311 us
    reduce_scatter x1, waiting for transfers between devices, on_device(): lax.psum_scatter(attn_local, 'seq', scatter_dimension=2, tiled=True)  144 us
    all_to_all x1, waiting for transfers between devices, on_device(): lax.all_to_all(qkv.reshape(seq_local, shard_len, 3, model_width), 'seq',...  79.6 us
    all_gather x1, waiting for transfers between devices, on_device(): lax.all_gather(ffn_rows, 'seq', axis=2, tiled=True)  57.1 us
    reduce_scatter x1, waiting for transfers between devices, on_device(): lax.psum_scatter(ffn_part, 'fsdp', scatter_dimension=1, tiled=True)  49.9 us
    all_gather x1, waiting for transfers between devices, on_device(): lax.all_gather(attn_rows, 'seq', axis=2, tiled=True)  47.7 us
    all_to_all x1, waiting for transfers between devices, on_device(): lax.all_to_all(grad_stack, 'seq', split_axis=1, concat_axis=3, tiled=True)  44.5 us
    unnamed x90, local copies, waits for them, and re-layouts  43.9 us
  transfers between devices with their start and end apart: 12, of which 12 were waited for; matrix products, arithmetic and copies ran while one was open for 8% of the time, Pallas kernels for 0%

commit v1 on v0

--- a/solution.py
+++ b/solution.py
@@ -3,6 +3,7 @@
 import jax.numpy as jnp
 from jax import lax
 from jax.sharding import PartitionSpec as P
+from jax.lax import all_to_all, axis_size
 
 HEAD = 64
 STEP = 3
@@ -168,13 +169,11 @@
         jnp.einsum("rd,kde->rke", token_rows, attn_w[:3], preferred_element_type=jnp.float32)
         + bias_qkv
     ).astype(jnp.bfloat16)
-    qkv_heads = lax.all_to_all(
-        qkv.reshape(seq_local, shard_len, 3, model_width),
-        "seq",
-        split_axis=3,
-        concat_axis=1,
-        tiled=True,
-    )
+    field = qkv.reshape(seq_local, shard_len, 3, model_width)
+    a_now = jnp.split(field, axis_size("seq"), axis=3)
+    response = jnp.stack(a_now)
+    now = all_to_all(response, axis_name="seq", split_axis=0, concat_axis=0)
+    qkv_heads = jnp.concatenate(now, axis=1)
     mixed_heads, log_total = attend_all(qkv_heads, lengths)
     mixed_local = lax.all_to_all(mixed_heads, "seq", split_axis=1, concat_axis=2, tiled=True)
     mixed_rows = mixed_local.reshape(row_count, model_width)

time: 1120 us -> 1110 us (level)
    all_to_all x1, waiting for transfers between devices: 79.6 us -> 61.9 us  [on_device(): now = all_to_all(response, axis_name='seq', split_axis=0, concat_axis=0)]
    unnamed x90 -> x94, local copies, waits for them, and re-layouts: 43.9 us -> 44.5 us
where the time goes in v1:
time: 1110 us
  waiting for transfers between devices  832 us (75%)
  blocking collectives  79.5 us (7%)
  local copies, waits for them, and re-layouts  76.7 us (7%)
  matrix products  48.4 us (4%)
  other arithmetic  41.2 us (4%)
  between operations  16.1 us (1%)
  starting transfers between devices  11.5 us (1%)
    reduce_scatter x1, waiting for transfers between devices, on_device(): lax.psum_scatter(ffn_local, 'seq', scatter_dimension=2, tiled=True)  311 us
    reduce_scatter x1, waiting for transfers between devices, on_device(): lax.psum_scatter(attn_local, 'seq', scatter_dimension=2, tiled=True)  144 us
    all_gather x1, waiting for transfers between devices, on_device(): lax.all_gather(ffn_rows, 'seq', axis=2, tiled=True)  67.9 us
    all_to_all x1, waiting for transfers between devices, on_device(): now = all_to_all(response, axis_name='seq', split_axis=0, concat_axis=0)  61.9 us
    reduce_scatter x1, waiting for transfers between devices, on_device(): lax.psum_scatter(ffn_part, 'fsdp', scatter_dimension=1, tiled=True)  49.8 us
    all_gather x1, waiting for transfers between devices, on_device(): lax.all_gather(attn_rows, 'seq', axis=2, tiled=True)  47.7 us
    unnamed x94, local copies, waits for them, and re-layouts  44.5 us
    all_to_all x1, waiting for transfers between devices, on_device(): lax.all_to_all(grad_stack, 'seq', split_axis=1, concat_axis=3, tiled=True)  44.5 us
  transfers between devices with their start and end apart: 12, of which 12 were waited for; matrix products, arithmetic and copies ran while one was open for 8% of the time, Pallas kernels for 0%

profile of v1, /device:TPU:0, one launch (start us, length us, event | category | flops | bytes accessed | tf_op | source)
XLA Modules:
  0.0 1105.3 jit_solution(16055257712252431222)
XLA Ops:
  11.1 27.6 %all-gather.6.cloned.1.call-done = bf16[4,768,192]{2,0,1:T(4,128)(2,1)} async-done(((bf16[4,96,192]{2,0,1:T(4,128)(2,1)}), bf16[4,768,192]{2,0,1:T(4,128)(2,1)}) %all-gather.6.cloned.1.call-update) | async-done | bytes 1179664 | tf_op jit(solution)/shard_map/all_gather | solution.py:154
  38.8 4.2 copy.147
  43.0 27.2 %all-gather.10.cloned.1.call-done = bf16[2,768,768]{2,1,0:T(8,128)(2,1)} async-done(((bf16[2,96,768]{2,1,0:T(8,128)(2,1)}), bf16[2,768,768]{2,1,0:T(8,128)(2,1)}) %all-gather.10.cloned.1.call-update) | async-done | bytes 2359312 | tf_op jit(solution)/shard_map/all_gather | solution.py:155
  70.2 42.6 %all-gather = bf16[32,24,12]{1,2,0:T(8,128)(2,1)S(1)} all-gather(bf16[1,24,12]{1,2,0:T(8,128)(2,1)S(1)} %convert_bitcast_fusion.1), channel_id=1, replica_groups=mesh['seq'=4,'fsdp'=8] {'seq','fsdp'}, dimensions={0}, use_global_device_ids=true | all-gather | bytes 19008 | tf_op jit(solution)/shard_map/all_gather | solution.py:157
  113.8 47.7 %all-gather.8.cloned.1.call-done = bf16[4,768,768]{1,0,2:T(4,128)(2,1)} async-done(((bf16[4,768,192]{1,0,2:T(4,128)(2,1)}), bf16[4,768,768]{1,0,2:T(4,128)(2,1)}) %all-gather.8.cloned.1.call-update) | async-done | bytes 4718608 | tf_op jit(solution)/shard_map/all_gather | solution.py:165
  161.5 6.5 copy.195
  168.0 2.4 fusion.12
  172.7 3.7 all-to-all-start
  177.1 61.9 %all-to-all-done = bf16[4,1,256,3,192]{2,4,3,1,0:T(8,128)(2,1)S(1)} async-done(((bf16[4,1,256,3,192]{2,4,3,1,0:T(8,128)(2,1)}), bf16[4,1,256,3,192]{2,4,3,1,0:T(8,128)(2,1)S(1)}, u32[]{:S(2)}, u32[]{:S(2)}) %all-to-all-start) | async-done | bytes 1179680 | tf_op jit(solution)/shard_map/all_to_all | solution.py:175
  240.8 2.3 fusion.1
  243.2 3.2 exponential_reduce_fusion
  247.7 3.0 fusion
  254.8 4.0 reduce.14
  260.2 3.7 all-to-all-start.1
  264.0 6.2 slice.101
  270.2 5.4 copy.196
  275.7 11.7 %all-to-all-done.1 = bf16[4,2,24576]{2,1,0:T(2,128)(2,1)S(1)} async-done(((bf16[4,2,24576]{2,1,0:T(2,128)(2,1)}), bf16[4,2,24576]{2,1,0:T(2,128)(2,1)S(1)}, u32[]{:S(2)}, u32[]{:S(2)}) %all-to-all-start.1) | async-done | bytes 393248 | tf_op jit(solution)/shard_map/all_to_all | solution.py:178
  289.3 2.3 copy.154
  293.8 67.9 %all-gather.12.cloned.1.call-done = bf16[2,768,3072]{2,1,0:T(8,128)(2,1)} async-done(((bf16[2,768,768]{2,1,0:T(8,128)(2,1)}), bf16[2,768,3072]{2,1,0:T(8,128)(2,1)}) %all-gather.12.cloned.1.call-update) | async-done | bytes 9437200 | tf_op jit(solution)/shard_map/all_gather | solution.py:166
  361.7 3.7 multiply_convert_fusion.1
  370.8 2.5 fusion.53
  377.5 2.6 copy.157
  380.1 3.0 reduce.15
  383.2 14.5 %all_to_all.50 = bf16[4,2,24576]{2,1,0:T(2,128)(2,1)S(1)} all-to-all(bf16[4,2,24576]{2,1,0:T(2,128)(2,1)S(1)} %reshape.193), channel_id=1, replica_groups=mesh['seq'=4,'fsdp'=8] {'seq'}, dimensions={0} | all-to-all | bytes 786432 | tf_op jit(solution)/shard_map/all_to_all | solution.py:200
  398.8 5.6 convolution_convert_fusion
  404.6 7.1 multiply_convert_fusion
  411.7 2.8 fusion.20
  417.3 2.4 copy.164
  419.7 3.5 copy.163
  423.2 6.0 maximum_bitcast_fusion
  429.2 3.6 all-to-all-start.3
  433.1 3.0 convolution_bitcast_fusion.3
  436.1 44.5 %all-to-all-done.3 = bf16[1,1024,3,192]{3,2,0,1:T(4,128)(2,1)S(1)} async-done(((bf16[1,1024,3,192]{3,2,0,1:T(4,128)(2,1)}), bf16[1,1024,3,192]{3,2,0,1:T(4,128)(2,1)S(1)}, u32[]{:S(2)}, u32[]{:S(2)}) %all-to-all-start.3) | async-done | bytes 1179680 | tf_op jit(solution)/shard_map/all_to_all | solution.py:208
  481.9 3.9 copy.187
  488.1 4.3 pad_maximum_fusion.1
  493.6 2.9 convolution_bitcast_fusion
  498.1 7.0 pad_maximum_fusion
  508.4 144.4 %reduce-scatter.11.cloned.1.call-done = f32[4,768,192]{1,2,0:T(8,128)} async-done(((f32[4,768,768]{1,2,0:T(8,128)}), f32[4,768,192]{1,2,0:T(8,128)}) %reduce-scatter.11.cloned.1.call-update) | async-done | bytes 2359312 | tf_op jit(solution)/shard_map/reduce_scatter | solution.py:247
  652.8 3.1 copy.188
  655.9 3.1 reshape.177
  659.2 310.8 %reduce-scatter.13.cloned.1.call-done = f32[2,768,768]{2,1,0:T(8,128)} async-done(((f32[2,768,3072]{2,1,0:T(8,128)}), f32[2,768,768]{2,1,0:T(8,128)}) %reduce-scatter.13.cloned.1.call-update) | async-done | bytes 4718608 | tf_op jit(solution)/shard_map/reduce_scatter | solution.py:248
  972.5 4.0 fusion.18
  976.5 18.1 %reduce-scatter.19.cloned.1.call-done = f32[192,12]{1,0:T(8,128)} async-done(((f32[768,12]{1,0:T(8,128)}), f32[192,12]{1,0:T(8,128)}) %reduce-scatter.19.cloned.1.call-update) | async-done | bytes 9232
  995.6 22.3 %all-reduce = f32[12,192]{1,0:T(8,128)S(1)} all-reduce(f32[12,192]{1,0:T(8,128)S(1)} %copy.191), channel_id=7, replica_groups=mesh['seq'=4,'fsdp'=8] {'fsdp'}, use_global_device_ids=true, to_apply=%region_24.25.clone | all-reduce | flops 2304 | bytes 18432
  1018.6 20.0 %reduce-scatter.17.cloned.1.call-done = f32[96,768]{1,0:T(8,128)} async-done(((f32[768,768]{1,0:T(8,128)}), f32[96,768]{1,0:T(8,128)}) %reduce-scatter.17.cloned.1.call-update) | async-done | bytes 294928
  1041.1 2.0 copy.176
  1046.0 49.8 %reduce-scatter.15.cloned.1.call-done = f32[2,96,768]{2,1,0:T(8,128)} async-done(((f32[2,768,768]{2,1,0:T(8,128)}), f32[2,96,768]{2,1,0:T(8,128)}) %reduce-scatter.15.cloned.1.call-update) | async-done | bytes 589840 | tf_op jit(solution)/shard_map/reduce_scatter | solution.py:253
  1095.8 2.8 multiply_subtract_fusion
  (171 shorter events, 52.0 us)
Async XLA Ops:
  7.2 31.6 %all-gather.6.cloned.1.call-start = ((), (), s32[]{:S(2)}) async-start(), calls=%async_computation.9 | async-start | bytes 1769472 | tf_op jit(solution)/shard_map/all_gather | solution.py:154
  9.2 61.0 %all-gather.10.cloned.1.call-start = ((), (), s32[]{:S(2)}) async-start(), calls=%async_computation.11 | async-start | bytes 2654208 | tf_op jit(solution)/shard_map/all_gather | solution.py:155
  11.1 59.1 %copy-start.30 = (f32[12,24]{1,0:T(8,128)S(1)}, f32[12,24]{1,0:T(8,128)}, u32[]{:S(2)}) copy-start(f32[12,24]{1,0:T(8,128)} %param.21) | copy-start | bytes 3460
  11.1 150.4 %all-gather.8.cloned.1.call-start = ((), (), s32[]{:S(2)}) async-start(), calls=%async_computation.10 | async-start | bytes 5898240 | tf_op jit(solution)/shard_map/all_gather | solution.py:165
  43.0 318.8 %all-gather.12.cloned.1.call-start = ((), (), s32[]{:S(2)}) async-start(), calls=%async_computation.12 | async-start | bytes 11796480 | tf_op jit(solution)/shard_map/all_gather | solution.py:166
  113.0 48.4 %copy-start.28 = (bf16[768,12]{0,1:T(8,128)(2,1)}, bf16[768,12]{0,1:T(8,128)(2,1)S(1)}, u32[]{:S(2)}) copy-start(bf16[768,12]{0,1:T(8,128)(2,1)S(1)} %reshape.174) | copy-start | bytes 55300
  168.0 2.4 copy-start.12
  172.7 66.3 %all-to-all-start = ((bf16[4,1,256,3,192]{2,4,3,1,0:T(8,128)(2,1)}), bf16[4,1,256,3,192]{2,4,3,1,0:T(8,128)(2,1)S(1)}, u32[]{:S(2)}, u32[]{:S(2)}) async-start(bf16[4,1,256,3,192]{2,4,3,1,0:T(8,128)(2,1)} %copy.150), calls=%async_computation | async-start | bytes 2359296 | tf_op jit(solution)/shard_map/all_to_all | solution.py:175
  240.8 9.9 copy-start.17
  243.2 4.6 copy-start
  250.8 2.7 copy-start.1
  253.5 10.6 copy-start.10
  253.5 10.4 copy-start.29
  260.2 27.2 %all-to-all-start.1 = ((bf16[4,2,24576]{2,1,0:T(2,128)(2,1)}), bf16[4,2,24576]{2,1,0:T(2,128)(2,1)S(1)}, u32[]{:S(2)}, u32[]{:S(2)}) async-start(bf16[4,2,24576]{2,1,0:T(2,128)(2,1)} %reshape.191), calls=%async_computation.1 | async-start | bytes 786432 | tf_op jit(solution)/shard_map/all_to_all | solution.py:178
  361.7 5.7 copy-start.33
  365.5 3.5 copy-start.21
  367.4 1.8 copy-start.8
  370.8 2.5 copy-start.13
  373.3 1.7 copy-start.22
  375.3 0.9 copy-start.4
  398.8 5.7 copy-start.11
  398.8 5.8 copy-start.18
  414.4 2.0 copy-start.20
  429.2 51.4 %all-to-all-start.3 = ((bf16[1,1024,3,192]{3,2,0,1:T(4,128)(2,1)}), bf16[1,1024,3,192]{3,2,0,1:T(4,128)(2,1)S(1)}, u32[]{:S(2)}, u32[]{:S(2)}) async-start(bf16[1,1024,3,192]{3,2,0,1:T(4,128)(2,1)} %maximum_bitcast_fusion), calls=%async_computation.3 | async-start | bytes 4194304 | tf_op jit(solution)/shard_map/all_to_all | solution.py:208
  432.8 220.0 %reduce-scatter.11.cloned.1.call-start = ((), (), s32[]{:S(2)}) async-start(), calls=%async_computation.13 | async-start | bytes 11796480 | tf_op jit(solution)/shard_map/reduce_scatter | solution.py:247
  436.1 49.9 %copy-start.16 = (bf16[1,256,768]{2,1,0:T(8,128)(2,1)S(1)}, bf16[1,256,768]{2,1,0:T(8,128)(2,1)}, u32[]{:S(2)}) copy-start(bf16[1,256,768]{2,1,0:T(8,128)(2,1)} %param.12) | copy-start | bytes 1179652
  480.6 1.3 copy-start.3
  486.0 1.1 copy-start.6
  486.0 2.1 copy-start.2
  492.4 1.1 copy-start.14
  492.5 477.5 %reduce-scatter.13.cloned.1.call-start = ((), (), s32[]{:S(2)}) async-start(), calls=%async_computation.14 | async-start | bytes 23592960 | tf_op jit(solution)/shard_map/reduce_scatter | solution.py:248
  493.6 3.0 copy-start.23
  505.1 1.0 copy-start.9
  505.1 489.5 %reduce-scatter.19.cloned.1.call-start = ((), (), s32[]{:S(2)}) async-start(), calls=%async_computation.17 | async-start | bytes 491520
  508.3 530.2 %reduce-scatter.17.cloned.1.call-start = ((), (), s32[]{:S(2)}) async-start(), calls=%async_computation.16 | async-start | bytes 2654208
  659.1 310.9 %copy-start.19 = (f32[4,96,192]{2,1,0:T(8,128)S(1)}, f32[4,96,192]{2,1,0:T(8,128)}, u32[]{:S(2)}) copy-start(f32[4,96,192]{2,1,0:T(8,128)} %param.15) | copy-start | bytes 884740
  659.1 311.1 %copy-start.26 = (f32[4,96,192]{2,1,0:T(8,128)S(1)}, f32[4,96,192]{2,1,0:T(8,128)}, u32[]{:S(2)}) copy-start(f32[4,96,192]{2,1,0:T(8,128)} %param.16) | copy-start | bytes 884740
  659.1 436.7 %reduce-scatter.15.cloned.1.call-start = ((), (), s32[]{:S(2)}) async-start(), calls=%async_computation.15 | async-start | bytes 5308416 | tf_op jit(solution)/shard_map/reduce_scatter | solution.py:253
  970.0 1.0 copy-start.27
  970.0 1.2 copy-start.34
  970.0 2.4 copy-start.5
  970.0 2.4 copy-start.7
  972.4 45.5 %copy-start.31 = (f32[12,24]{1,0:T(8,128)S(1)}, f32[12,24]{1,0:T(8,128)}, u32[]{:S(2)}) copy-start(f32[12,24]{1,0:T(8,128)} %param.22) | copy-start | bytes 3460
  972.4 45.4 %copy-start.32 = (f32[12,24]{1,0:T(8,128)S(1)}, f32[12,24]{1,0:T(8,128)}, u32[]{:S(2)}) copy-start(f32[12,24]{1,0:T(8,128)} %param.23) | copy-start | bytes 3460
  1040.0 55.7 %copy-start.15 = (f32[2,96,768]{2,1,0:T(8,128)S(1)}, f32[2,96,768]{2,1,0:T(8,128)}, u32[]{:S(2)}) copy-start(f32[2,96,768]{2,1,0:T(8,128)} %param.18) | copy-start | bytes 1769476
  1041.1 54.7 %copy-start.24 = (f32[2,96,768]{2,1,0:T(8,128)S(1)}, f32[2,96,768]{2,1,0:T(8,128)}, u32[]{:S(2)}) copy-start(f32[2,96,768]{2,1,0:T(8,128)} %param.19) | copy-start | bytes 1769476
  1041.1 54.7 %copy-start.25 = (f32[2,96,768]{2,1,0:T(8,128)S(1)}, f32[2,96,768]{2,1,0:T(8,128)}, u32[]{:S(2)}) copy-start(f32[2,96,768]{2,1,0:T(8,128)} %param.20) | copy-start | bytes 1769476
Sparse Core Ops, SparseCore 0:
  10.4 28.2 all-gather.5
  41.2 28.8 all-gather.9
  71.7 89.6 all-gather.7
  162.9 198.8 all-gather.11
  492.6 160.2 reduce-scatter.10
  655.1 314.8 reduce-scatter.12
  972.8 21.7 reduce-scatter.18
  997.9 40.5 reduce-scatter.16
  1042.0 53.7 reduce-scatter.14
